TPU v7x, 256 devices: a whole 4x4x8 slice. The times are simulated.
256 devices in a mesh: col: 64 (over z, x, core), row: 4 (over y).
Axes of the slice: x: 4, y: 4, z: 8, core: 2. Of those that a mesh axis runs over, the one named last changes fastest.
Arguments:
- matrix: float32 [16, 512, 1, 8192], P(None, 'row', None, 'col'), may hold values from -1 to 5, as said below
- inverse_factors: float32 [2, 512, 512], replicated, may hold values from -1 to 1, as said below
Outputs:
- factored: float32 [16, 512, 1, 8192], P(None, 'row', None, 'col')
Inputs may be any that keep to these rules, and one draw needn't show every extreme that they name: matrix holds a symmetric matrix. Each inverse_factors[k] is lower triangular with a positive diagonal; it is given independently of matrix.
All inputs are finite; a program needn't handle non-finite values.
Results may differ from a plain program's by a relative error of at most 0.0001.
Values sent between devices are 32-bit elements; how exact they have to be, the bound alone decides.
No kernel may reach another device: no remote copies, remote signals or barrier semaphores. Data moves between devices by JAX's collectives and lax.ppermute only.
A program may use at most 64 MiB of HBM per device.

v0:
```python
import jax
import jax.numpy as jnp
from jax import lax
from jax.sharding import PartitionSpec as P


def broadcast(x, axis, root):
    mine = lax.axis_index(axis) == root
    return lax.psum(jnp.where(mine, x, jnp.zeros_like(x)), axis)


def exact_dot(left_side, right_side):
    return jnp.dot(
        left_side, right_side, precision=lax.Precision.HIGHEST, preferred_element_type=jnp.float32
    )


def shards(matrix, inverse_factors):
    col_count = lax.axis_size("col")
    row_count = lax.axis_size("row")
    col_index = lax.axis_index("col")
    row_index = lax.axis_index("row")
    row_blocks, block_cols, cycles, _ = matrix.shape
    panel_width = inverse_factors.shape[1]
    per_panel = panel_width // block_cols
    local_rows = row_blocks * block_cols
    square_view = matrix.reshape(local_rows, cycles * block_cols)
    global_rows = (
        (jnp.arange(row_blocks)[:, None] * row_count + row_index) * block_cols
        + jnp.arange(block_cols)[None, :]
    ).reshape(-1)
    take_index = (jnp.arange(cycles) * col_count + col_index) // row_count
    row_root = col_index % row_count

    def masked(factor_cols, offset):
        return jnp.where(global_rows[:, None] >= offset, factor_cols, 0.0)

    current = square_view
    for panel in range(2):
        factor = inverse_factors[panel]
        pieces = [
            broadcast(current, "col", panel * per_panel + member) for member in range(per_panel)
        ]
        factor_cols = exact_dot(jnp.concatenate(pieces, axis=1), factor.T)
        trailing = masked(factor_cols, (panel + 1) * panel_width)
        blocked = trailing.reshape(row_blocks, block_cols, panel_width)
        picked = jnp.take(blocked, take_index, axis=0).reshape(cycles * block_cols, panel_width)
        gathered = lax.all_gather(picked, "row", axis=0, tiled=True)
        column_part = lax.dynamic_slice_in_dim(
            gathered, row_root * picked.shape[0], picked.shape[0], 0
        )
        current = current - exact_dot(trailing, column_part.T)
        place_factor_cols = masked(factor_cols, panel * panel_width)
        offset_id = col_index - panel * per_panel
        inside = (offset_id >= 0) & (offset_id < per_panel)
        position = jnp.clip(offset_id, 0, per_panel - 1)
        chosen = lax.dynamic_slice_in_dim(place_factor_cols, position * block_cols, block_cols, 1)
        leading = jnp.where(inside, chosen, current)
        current = jnp.concatenate([leading, current[:, block_cols:]], axis=1)
    return current.reshape(row_blocks, block_cols, cycles, block_cols)


def solution(mesh):
    return jax.shard_map(
        shards,
        mesh=mesh,
        in_specs=(P(None, "row", None, "col"), P()),
        out_specs=P(None, "row", None, "col"),
        check_vma=False,
    )
```

profile of v0, /device:TPU:2, one launch (start us, length us, event | category | flops | bytes accessed | tf_op | source)
XLA Modules:
  0.0 504.0 jit_solution(6828557385005431134)
XLA Ops:
  6.5 0.0 all-reduce.7.cloned.1.call-start
  6.5 0.0 copy-start.3
  6.5 3.4 broadcast_select_fusion.9
  10.0 0.0 all-reduce.7.cloned.1.call-update
  10.0 0.0 all-gather.5.cloned.1.call-start
  10.1 0.1 fusion.31
  10.2 199.4 %all-reduce.7.cloned.1.call-done = (f32[2048,128]{1,0:T(8,128)}, f32[2048,128]{1,0:T(8,128)}, f32[2048,128]{1,0:T(8,128)}, f32[2048,128]{1,0:T(8,128)}) async-done(((f32[2048,128]{1,0:T(8,128)}, f32[2048,128]{1,0:T(8,128)}, f32[2048,128]{1,0:T(8,128)}, f32[2048,128]{1,0:T(8,128)}), (f32[2048,128]{1,0:T(8,128)}, f32[2048,128]{1,0:T(8,128)}, f32[2048,128]{1,0:T(8,128)}, ...) | async-done | bytes 4194320 | tf_op jit(solution)/shard_map/psum | solution.py:9
  209.6 0.0 copy-done.3
  209.6 0.0 copy-start.2
  209.6 9.9 %broadcast_select_fusion = (f32[2048,512]{1,0:T(8,128)S(1)}, f32[2048,512]{1,0:T(8,128)}) fusion(pred[2048]{0:T(1024)(128)(4,1)S(1)} %get-tuple-element.35, f32[2,512,512]{2,1,0:T(8,128)S(1)} %copy-done.3, f32[2048,128]{1,0:T(8,128)} %get-tuple-element.21, f32[2048,128]{1,0:T(8,128)} %get-tuple-element.22, f32[2048,128]{1,0:T(8,128)} %get-tuple-element.23, ...), kind=kOutput, calls=%fused_computation.20 | convolution fusion | flops 6446645248 | bytes 13633536 | tf_op jit(solution)/shard_map/dot_general | solution.py:13
  219.5 0.0 copy-start
  219.5 2.0 copy-done
  221.5 0.7 dynamic-slice_select_fusion.3
  222.2 0.0 all-gather.5.cloned.1.call-update
  222.2 0.0 all-reduce.5.cloned.1.call-start
  222.3 25.7 %all-gather.5.cloned.1.call-done = f32[1,512,512]{2,1,0:T(8,128)} async-done(((f32[1,128,512]{2,1,0:T(8,128)}), f32[1,512,512]{2,1,0:T(8,128)}) %all-gather.5.cloned.1.call-update) | async-done | bytes 1048592 | tf_op jit(solution)/shard_map/all_gather | solution.py:48
  248.0 0.0 copy-done.2
  248.0 8.0 %broadcast_select_fusion.5 = (f32[2048,128]{1,0:T(8,128)}, f32[2048,128]{1,0:T(8,128)}, f32[2048,128]{1,0:T(8,128)}, f32[2048,128]{1,0:T(8,128)}, f32[2048,128]{1,0:T(8,128)S(1)}) fusion(pred[]{:T(512)S(6)} %eq.26, pred[]{:T(512)S(6)} %eq.33, pred[]{:T(512)S(6)} %eq.32, pred[]{:T(512)S(6)} %eq.31, f32[2048,128]{1,0:T(8,128)S(1)} %bitcast.40, ...), kind=kOutput, calls=%fused_computation.31 | convolution fusion | flops 1612447744 | bytes 11798541 | tf_op jit(solution)/shard_map/dot_general | solution.py:13
  256.0 0.0 all-reduce.5.cloned.1.call-update
  256.0 0.2 all-gather.7.cloned.1.call-start
  256.3 195.5 %all-reduce.5.cloned.1.call-done = (f32[2048,128]{1,0:T(8,128)}, f32[2048,128]{1,0:T(8,128)}, f32[2048,128]{1,0:T(8,128)}, f32[2048,128]{1,0:T(8,128)}) async-done(((f32[2048,128]{1,0:T(8,128)}, f32[2048,128]{1,0:T(8,128)}, f32[2048,128]{1,0:T(8,128)}, f32[2048,128]{1,0:T(8,128)}), (f32[2048,128]{1,0:T(8,128)}, f32[2048,128]{1,0:T(8,128)}, f32[2048,128]{1,0:T(8,128)}, ...) | async-done | bytes 4194320 | tf_op jit(solution)/shard_map/psum | solution.py:9
  451.7 10.3 %broadcast_select_fusion.1 = (f32[2048,512]{1,0:T(8,128)S(1)}, f32[2048,512]{1,0:T(8,128)}) fusion(pred[2048]{0:T(1024)(128)(4,1)S(1)} %get-tuple-element.33, f32[2,512,512]{2,1,0:T(8,128)} %param.5, f32[2048,128]{1,0:T(8,128)} %get-tuple-element.17, f32[2048,128]{1,0:T(8,128)} %get-tuple-element.18, f32[2048,128]{1,0:T(8,128)} %get-tuple-element.19, ...), kind=kOutput, calls=%fused_computation.21 | convolution fusion | flops 6446645248 | bytes 13633536 | tf_op jit(solution)/shard_map/dot_general | solution.py:13
  462.0 0.0 copy-start.1
  462.0 2.0 copy-done.1
  464.0 0.7 dynamic-slice_select_fusion.2
  464.7 0.0 all-gather.7.cloned.1.call-update
  464.8 25.7 %all-gather.7.cloned.1.call-done = f32[1,512,512]{2,1,0:T(8,128)} async-done(((f32[1,128,512]{2,1,0:T(8,128)}), f32[1,512,512]{2,1,0:T(8,128)}) %all-gather.7.cloned.1.call-update) | async-done | bytes 1048592 | tf_op jit(solution)/shard_map/all_gather | solution.py:48
  490.5 7.0 %fusion.16 = f32[2048,128]{1,0:T(8,128)} fusion(f32[2048,128]{1,0:T(8,128)S(1)} %get-tuple-element.38, f32[2048,512]{1,0:T(8,128)} %copy-done.1, f32[2048,512]{1,0:T(8,128)} %get-tuple-element.40, s32[]{:T(128)S(6)} %select_n.137, pred[2048]{0:T(1024)(128)(4,1)S(1)} %get-tuple-element.35, pred[]{:T(512)S(6)} %and.21, ...), kind=kOutput, calls=%fused_computation.17 | convolution fusion | flops 1611399168 | bytes 7604233 | tf_op jit(solution)/shard_map/dot_general | solution.py:13
  (1 shorter events, 0.0 us)
Async XLA Ops:
  6.5 203.1 %all-reduce.7.cloned.1.call-start = ((), (), s32[]{:S(2)}) async-start(), calls=%async_computation.3 | async-start | bytes 8388608 | tf_op jit(solution)/shard_map/psum | solution.py:9
  6.5 203.1 %copy-start.3 = (f32[2,512,512]{2,1,0:T(8,128)S(1)}, f32[2,512,512]{2,1,0:T(8,128)}, u32[]{:S(2)}) copy-start(f32[2,512,512]{2,1,0:T(8,128)} %param.5) | copy-start | bytes 6291460
  10.0 238.0 %all-gather.5.cloned.1.call-start = ((), (), s32[]{:S(2)}) async-start(), calls=%async_computation | async-start | bytes 1310720 | tf_op jit(solution)/shard_map/all_gather | solution.py:48
  209.6 38.4 %copy-start.2 = (f32[16,128,1,128]{3,2,1,0:T(1,128)S(1)}, f32[16,128,1,128]{3,2,1,0:T(1,128)}, u32[]{:S(2)}) copy-start(f32[16,128,1,128]{3,2,1,0:T(1,128)} %param.4) | copy-start | bytes 3145732
  219.5 2.0 copy-start
  222.2 229.5 %all-reduce.5.cloned.1.call-start = ((), (), s32[]{:S(2)}) async-start(), calls=%async_computation.2 | async-start | bytes 8388608 | tf_op jit(solution)/shard_map/psum | solution.py:9
  256.0 234.5 %all-gather.7.cloned.1.call-start = ((), (), s32[]{:S(2)}) async-start(), calls=%async_computation.1 | async-start | bytes 1310720 | tf_op jit(solution)/shard_map/all_gather | solution.py:48
  462.0 2.0 copy-start.1
Sparse Core Ops, SparseCore 0:
  11.3 198.2 all-reduce.6
  222.3 25.5 all-gather.4
  256.1 195.5 all-reduce.4
  464.9 25.5 all-gather.6
where the time goes:
time: 504 us
  waiting for transfers between devices  446 us (88%)
  matrix products  35.2 us (7%)
  between operations  13.2 us (3%)
    psum x2, waiting for transfers between devices, broadcast(): return lax.psum(jnp.where(mine, x, jnp.zeros_like(x)), axis)  395 us
    all_gather x2, waiting for transfers between devices, shards(): gathered = lax.all_gather(picked, 'row', axis=0, tiled=True)  51.4 us
    dot_general x4, matrix products, exact_dot(): jnp.dot(left_side, right_side, precision=lax.Precision.HIGHEST, preferred...  35.2 us
  transfers between devices with their start and end apart: 4, of which 4 were waited for; matrix products, arithmetic and copies ran while one was open for 0% of the time, Pallas kernels for 0%

commit v1 on v0

--- a/solution.py
+++ b/solution.py
@@ -2,6 +2,14 @@
 import jax.numpy as jnp
 from jax import lax
 from jax.sharding import PartitionSpec as P
+
+
+def gather_from_all(value, axis, dim):
+    size = lax.axis_size(axis)
+    repeats = [size if d == dim else 1 for d in range(value.ndim)]
+    return lax.all_to_all(
+        jnp.tile(value, repeats), axis, split_axis=dim, concat_axis=dim, tiled=True
+    )
 
 
 def broadcast(x, axis, root):
@@ -45,7 +53,7 @@
         trailing = masked(factor_cols, (panel + 1) * panel_width)
         blocked = trailing.reshape(row_blocks, block_cols, panel_width)
         picked = jnp.take(blocked, take_index, axis=0).reshape(cycles * block_cols, panel_width)
-        gathered = lax.all_gather(picked, "row", axis=0, tiled=True)
+        gathered = gather_from_all(picked, "row", 0)
         column_part = lax.dynamic_slice_in_dim(
             gathered, row_root * picked.shape[0], picked.shape[0], 0
         )

time: 504 us -> 487 us (0.966)
  waiting for transfers between devices: 446 us -> 420 us
  starting transfers between devices: 0.31 us -> 8.57 us
    all_gather x2 -> x0, waiting for transfers between devices: 51.4 us -> none  [shards(): gathered = lax.all_gather(picked, 'row', axis=0, tiled=True)]
    all_to_all x0 -> x2, waiting for transfers between devices: none -> 27.4 us  [gather_from_all(): lax.all_to_all(jnp.tile(value, repeats), axis, split_axis=dim, concat_axi...]
    all_to_all x0 -> x2, starting transfers between devices: none -> 8.57 us  [gather_from_all(): lax.all_to_all(jnp.tile(value, repeats), axis, split_axis=dim, concat_axi...]
where the time goes in v1:
time: 487 us; the launch traced here: 486 us
  waiting for transfers between devices  420 us (86%)
  matrix products  35 us (7%)
  between operations  13.4 us (3%)
  starting transfers between devices  8.57 us (2%)
  local copies, waits for them, and re-layouts  6.16 us (1%)
    psum x2, waiting for transfers between devices, broadcast(): return lax.psum(jnp.where(mine, x, jnp.zeros_like(x)), axis)  392 us
    dot_general x4, matrix products, exact_dot(): jnp.dot(left_side, right_side, precision=lax.Precision.HIGHEST, preferred...  35 us
    all_to_all x2, waiting for transfers between devices, gather_from_all(): lax.all_to_all(jnp.tile(value, repeats), axis, split_axis=dim, concat_axi...  27.4 us
  transfers between devices with their start and end apart: 4, of which 4 were waited for; matrix products, arithmetic and copies ran while one was open for 0% of the time, Pallas kernels for 0%

profile of v1, /device:TPU:2, one launch (start us, length us, event | category | flops | bytes accessed | tf_op | source)
XLA Modules:
  0.0 486.4 jit_solution(5711089034028160663)
XLA Ops:
  6.5 0.0 all-reduce.7.cloned.1.call-start
  6.5 0.0 copy-start.3
  6.5 3.4 broadcast_select_fusion.9
  10.0 0.0 all-reduce.7.cloned.1.call-update
  10.0 0.1 fusion.29
  10.1 199.5 %all-reduce.7.cloned.1.call-done = (f32[2048,128]{1,0:T(8,128)}, f32[2048,128]{1,0:T(8,128)}, f32[2048,128]{1,0:T(8,128)}, f32[2048,128]{1,0:T(8,128)}) async-done(((f32[2048,128]{1,0:T(8,128)}, f32[2048,128]{1,0:T(8,128)}, f32[2048,128]{1,0:T(8,128)}, f32[2048,128]{1,0:T(8,128)}), (f32[2048,128]{1,0:T(8,128)}, f32[2048,128]{1,0:T(8,128)}, f32[2048,128]{1,0:T(8,128)}, ...) | async-done | bytes 4194320 | tf_op jit(solution)/shard_map/psum | solution.py:17
  209.6 0.0 copy-done.3
  209.6 9.8 %broadcast_select_fusion = (f32[2048,512]{1,0:T(8,128)S(1)}, f32[2048,512]{1,0:T(8,128)}) fusion(pred[2048]{0:T(1024)(128)(4,1)S(1)} %get-tuple-element.35, f32[2,512,512]{2,1,0:T(8,128)S(1)} %copy-done.3, f32[2048,128]{1,0:T(8,128)} %get-tuple-element.21, f32[2048,128]{1,0:T(8,128)} %get-tuple-element.22, f32[2048,128]{1,0:T(8,128)} %get-tuple-element.23, ...), kind=kOutput, calls=%fused_computation.20 | convolution fusion | flops 6446645248 | bytes 13633536 | tf_op jit(solution)/shard_map/dot_general | solution.py:21
  219.4 0.0 copy-start
  219.4 0.0 copy-start.2
  219.4 2.0 copy-done
  221.4 1.1 tile.17
  222.5 4.3 all-to-all-start
  226.8 0.0 all-reduce.5.cloned.1.call-start
  226.8 13.7 %all-to-all-done = f32[4,128,512]{2,1,0:T(8,128)S(1)} async-done(((f32[4,128,512]{2,1,0:T(8,128)}), f32[4,128,512]{2,1,0:T(8,128)S(1)}, u32[]{:S(2)}, u32[]{:S(2)}) %all-to-all-start) | async-done | bytes 1048608 | tf_op jit(solution)/shard_map/all_to_all | solution.py:10
  240.5 0.0 copy-done.2
  240.5 8.0 %broadcast_select_fusion.5 = (f32[2048,128]{1,0:T(8,128)}, f32[2048,128]{1,0:T(8,128)}, f32[2048,128]{1,0:T(8,128)}, f32[2048,128]{1,0:T(8,128)}, f32[2048,128]{1,0:T(8,128)S(1)}) fusion(pred[]{:T(512)S(6)} %eq.26, pred[]{:T(512)S(6)} %eq.33, pred[]{:T(512)S(6)} %eq.32, pred[]{:T(512)S(6)} %eq.31, f32[2048,128]{1,0:T(8,128)S(1)} %bitcast.38, ...), kind=kOutput, calls=%fused_computation.31 | convolution fusion | flops 1612447744 | bytes 11798541 | tf_op jit(solution)/shard_map/dot_general | solution.py:21
  248.4 0.0 all-reduce.5.cloned.1.call-update
  248.5 192.9 %all-reduce.5.cloned.1.call-done = (f32[2048,128]{1,0:T(8,128)}, f32[2048,128]{1,0:T(8,128)}, f32[2048,128]{1,0:T(8,128)}, f32[2048,128]{1,0:T(8,128)}) async-done(((f32[2048,128]{1,0:T(8,128)}, f32[2048,128]{1,0:T(8,128)}, f32[2048,128]{1,0:T(8,128)}, f32[2048,128]{1,0:T(8,128)}), (f32[2048,128]{1,0:T(8,128)}, f32[2048,128]{1,0:T(8,128)}, f32[2048,128]{1,0:T(8,128)}, ...) | async-done | bytes 4194320 | tf_op jit(solution)/shard_map/psum | solution.py:17
  441.3 10.3 %broadcast_select_fusion.1 = (f32[2048,512]{1,0:T(8,128)S(1)}, f32[2048,512]{1,0:T(8,128)}) fusion(pred[2048]{0:T(1024)(128)(4,1)S(1)} %get-tuple-element.33, f32[2,512,512]{2,1,0:T(8,128)} %param.5, f32[2048,128]{1,0:T(8,128)} %get-tuple-element.17, f32[2048,128]{1,0:T(8,128)} %get-tuple-element.18, f32[2048,128]{1,0:T(8,128)} %get-tuple-element.19, ...), kind=kOutput, calls=%fused_computation.21 | convolution fusion | flops 6446645248 | bytes 13633536 | tf_op jit(solution)/shard_map/dot_general | solution.py:21
  451.6 0.0 copy-start.1
  451.6 2.0 copy-done.1
  453.6 1.1 tile.19
  454.7 4.3 all-to-all-start.1
  459.0 13.7 %all-to-all-done.1 = f32[4,128,512]{2,1,0:T(8,128)S(1)} async-done(((f32[4,128,512]{2,1,0:T(8,128)}), f32[4,128,512]{2,1,0:T(8,128)S(1)}, u32[]{:S(2)}, u32[]{:S(2)}) %all-to-all-start.1) | async-done | bytes 1048608 | tf_op jit(solution)/shard_map/all_to_all | solution.py:10
  472.7 6.9 %fusion.16 = f32[2048,128]{1,0:T(8,128)} fusion(f32[2048,128]{1,0:T(8,128)S(1)} %get-tuple-element.38, f32[2048,512]{1,0:T(8,128)} %copy-done.1, f32[2048,512]{1,0:T(8,128)} %get-tuple-element.40, s32[]{:T(128)S(6)} %select_n.137, pred[2048]{0:T(1024)(128)(4,1)S(1)} %get-tuple-element.35, pred[]{:T(512)S(6)} %and.21, f32[512,512]{1,0:T(8,128)S(1)} %bitcast.40, ...), kind=kOutput, calls=%fused_computation.17 | convolution fusion | flops 1611399168 | bytes 7604233 | tf_op jit(solution)/shard_map/dot_general | solution.py:21
  (3 shorter events, 0.0 us)
Async XLA Ops:
  6.5 203.1 %all-reduce.7.cloned.1.call-start = ((), (), s32[]{:S(2)}) async-start(), calls=%async_computation.3 | async-start | bytes 8388608 | tf_op jit(solution)/shard_map/psum | solution.py:17
  6.5 203.1 %copy-start.3 = (f32[2,512,512]{2,1,0:T(8,128)S(1)}, f32[2,512,512]{2,1,0:T(8,128)}, u32[]{:S(2)}) copy-start(f32[2,512,512]{2,1,0:T(8,128)} %param.5) | copy-start | bytes 6291460
  219.4 2.0 copy-start
  219.4 21.1 %copy-start.2 = (f32[16,128,1,128]{3,2,1,0:T(1,128)S(1)}, f32[16,128,1,128]{3,2,1,0:T(1,128)}, u32[]{:S(2)}) copy-start(f32[16,128,1,128]{3,2,1,0:T(1,128)} %param.4) | copy-start | bytes 3145732
  222.5 18.0 %all-to-all-start = ((f32[4,128,512]{2,1,0:T(8,128)}), f32[4,128,512]{2,1,0:T(8,128)S(1)}, u32[]{:S(2)}, u32[]{:S(2)}) async-start(f32[4,128,512]{2,1,0:T(8,128)} %tile.17), calls=%async_computation | async-start | bytes 2097152 | tf_op jit(solution)/shard_map/all_to_all | solution.py:10
  226.8 214.5 %all-reduce.5.cloned.1.call-start = ((), (), s32[]{:S(2)}) async-start(), calls=%async_computation.2 | async-start | bytes 8388608 | tf_op jit(solution)/shard_map/psum | solution.py:17
  451.6 2.0 copy-start.1
  454.7 18.0 %all-to-all-start.1 = ((f32[4,128,512]{2,1,0:T(8,128)}), f32[4,128,512]{2,1,0:T(8,128)S(1)}, u32[]{:S(2)}, u32[]{:S(2)}) async-start(f32[4,128,512]{2,1,0:T(8,128)} %tile.19), calls=%async_computation.1 | async-start | bytes 2097152 | tf_op jit(solution)/shard_map/all_to_all | solution.py:10
Sparse Core Ops, SparseCore 0:
  11.3 198.2 all-reduce.6
  248.6 192.6 all-reduce.4
